TPU v7x, 32 devices: a whole 2x2x4 slice. The times are simulated.
32 devices in a mesh: dp: 8 (over z, core), tp: 4 (over y, x).
Axes of the slice: x: 2, y: 2, z: 4, core: 2. Of those that a mesh axis runs over, the one named last changes fastest.
Arguments:
- x_in: bfloat16 [8192, 2048], P(('dp', 'tp')), may hold values from -6 to 6
- norm_gain: float32 [2048], replicated, may hold values from 0.5 to 1.5
- w_z: bfloat16 [2048, 4096], P(None, 'tp'), may hold values from -0.125 to 0.125
- w_x: bfloat16 [2048, 4096], P(None, 'tp'), may hold values from -0.125 to 0.125
- w_b: bfloat16 [2048, 128], P(None, 'tp'), may hold values from -0.125 to 0.125
- w_c: bfloat16 [2048, 128], P(None, 'tp'), may hold values from -0.125 to 0.125
- w_dt: bfloat16 [2048, 64], P(None, 'tp'), may hold values from -0.125 to 0.125
- conv_w: float32 [4352, 4], replicated, may hold values from -3 to 3
- conv_b: float32 [4352], replicated, may hold values from -3 to 3
- dt_bias: float32 [64], replicated, may hold values from -6 to -2
- a_log: float32 [64], replicated, may hold values from -2.5 to 0.5
- d_skip: float32 [64], replicated, may hold values from 0.5 to 1.5
- gate_gain: float32 [4096], replicated, may hold values from 0.5 to 1.5
- w_out: bfloat16 [4096, 2048], P('tp'), may hold values from -0.09375 to 0.09375
- doc_lens: int32 [8, 8], P('dp'), may hold values from 1 to 512, 1024 in all within a row
- d_out: bfloat16 [8192, 2048], P(('dp', 'tp')), may hold values from -6 to 6
Outputs:
- block_out: bfloat16 [8192, 2048], P(('dp', 'tp'))
- grad_x: float32 [8192, 2048], P(('dp', 'tp'))
- grad_norm_gain: float32 [2048], replicated
- grad_w_z: float32 [2048, 4096], P('dp', 'tp')
- grad_w_x: float32 [2048, 4096], P('dp', 'tp')
- grad_w_b: float32 [2048, 128], P('dp', 'tp')
- grad_w_c: float32 [2048, 128], P('dp', 'tp')
- grad_w_dt: float32 [2048, 64], P('dp', 'tp')
- grad_conv_w: float32 [4352, 4], replicated
- grad_conv_b: float32 [4352], replicated
- grad_dt_bias: float32 [64], replicated
- grad_a_log: float32 [64], replicated
- grad_d_skip: float32 [64], replicated
- grad_gate_gain: float32 [4096], replicated
- grad_w_out: float32 [4096, 2048], P('tp', 'dp')
Inputs may be any that keep to these rules, and one draw needn't show every extreme that they name: `doc_lens`: each row gives, in order, the lengths of the 8 documents packed into one sequence of 1024 tokens; a row sums to 1024 and its longest document has exactly 512 tokens.
All inputs are finite; a program needn't handle non-finite values.
Results may differ from a plain program's by a relative error of at most 0.012.
Values may be sent and summed in bfloat16 or wider, within the bound.
A program may use at most 256 MiB of HBM per device.

v0:
```python
import jax
import jax.numpy as jnp
from jax import lax
from jax.sharding import PartitionSpec as P

EPSILON = 1e-05
HIGHEST = lax.Precision.HIGHEST


def entering_2(array, axis, combine, identity, reverse):
    count, index = (lax.axis_size(axis), lax.axis_index(axis))
    everything = jax.tree.map(lambda part: lax.all_gather(part, axis), array)
    start = jax.tree.map(
        lambda part, zero: jnp.broadcast_to(jnp.asarray(zero, part.dtype), part.shape),
        array,
        identity,
    )

    def lap(k, before):
        at = count - 1 - k if reverse else k
        reached = at > index if reverse else at < index
        new = combine(before, jax.tree.map(lambda part: part[at], everything))
        return jax.tree.map(lambda a, b: jnp.where(reached, a, b), new, before)

    return lax.fori_loop(0, count, lap, start)


def span_parts(log_decay, segments, segment_prev):
    cumulative = jnp.cumsum(log_decay, axis=0)
    inward = jnp.exp(cumulative) * (segments == segment_prev).astype(jnp.float32)[:, None]
    carried = jnp.exp(cumulative[-1]) * (segments[-1] == segment_prev).astype(jnp.float32)
    return (cumulative, inward, carried)


def span_pass(state, values, b_rows, c_rows, log_decay, steps_dt, segments, segment_prev):
    cumulative, inward, carried = span_parts(log_decay, segments, segment_prev)
    length = segments.shape[0]
    order = jnp.arange(length, dtype=jnp.int32)
    same = (segments[:, None] == segments[None, :]) & (order[:, None] >= order[None, :])
    spread = cumulative[:, None, :] - cumulative[None, :, :]
    decays = jnp.exp(jnp.where(same[:, :, None], spread, -1e30))
    scores = jnp.dot(c_rows, b_rows.T, precision=HIGHEST)
    mixing = decays * scores[:, :, None] * steps_dt[None, :, :]
    output = jnp.einsum("tsh,shp->thp", mixing, values, precision=HIGHEST)
    output = (
        output + jnp.einsum("tn,hpn->thp", c_rows, state, precision=HIGHEST) * inward[:, :, None]
    )
    tail_same = segments == segments[-1]
    tail = (
        jnp.exp(jnp.where(tail_same[:, None], cumulative[-1][None, :] - cumulative, -1e30))
        * steps_dt
    )
    weighted = tail[:, :, None] * values
    state_out = carried[:, None, None] * state + jnp.einsum(
        "shp,sn->hpn", weighted, b_rows, precision=HIGHEST
    )
    return (output, state_out, carried)


def in_norm(values, gain):
    return (
        values
        * lax.rsqrt(jnp.mean(values * values, axis=-1, keepdims=True) + EPSILON)
        * gain[None, :]
    )


def combine(earlier, later):
    return (earlier[0] * later[0], later[0][:, None, None] * earlier[1] + later[1])


def body(
    x_in,
    norm_gain,
    w_z,
    w_x,
    w_b,
    w_c,
    w_dt,
    conv_w,
    conv_b,
    dt_bias,
    a_log,
    d_skip,
    gate_gain,
    w_out,
    doc_lens,
    d_out,
):
    tp_count = lax.axis_size("tp")
    tp_rank = lax.axis_index("tp")
    dev_rows = x_in.shape[0]
    group_rows = dev_rows * tp_count
    head_count = dt_bias.shape[0]
    inner_width = gate_gain.shape[0]
    head_size = inner_width // head_count
    state_size = (conv_w.shape[0] - inner_width) // 2
    rim_rows = conv_w.shape[1] - 1
    col_widths = [w_z.shape[1], w_x.shape[1], w_b.shape[1], w_c.shape[1], w_dt.shape[1]]
    col_edges = [0]
    for col_width in col_widths:
        col_edges.append(col_edges[-1] + col_width)
    total_cols = col_edges[-1]
    contract_first = (((0,), (0,)), ((), ()))
    contract_last = (((1,), (1,)), ((), ()))
    lengths = doc_lens[0]
    doc_starts = jnp.cumsum(lengths) - lengths
    positions = tp_rank * dev_rows - rim_rows + jnp.arange(dev_rows + rim_rows, dtype=jnp.int32)
    seg_ext = jnp.sum((positions[:, None] >= doc_starts[None, :]).astype(jnp.int32), axis=1)
    seg_own = seg_ext[rim_rows:]
    seg_before = [seg_ext[rim_rows - 1]]
    x_float = x_in.astype(jnp.float32)
    normed = in_norm(x_float, norm_gain).astype(jnp.bfloat16)
    w_joined = jnp.concatenate([w_z, w_x, w_b, w_c, w_dt], axis=1)
    gathered = lax.all_gather(normed, "tp", axis=0, tiled=True)
    projected = jnp.dot(gathered, w_joined, preferred_element_type=jnp.float32).astype(jnp.bfloat16)
    padded = jnp.concatenate([jnp.zeros((rim_rows, total_cols), jnp.bfloat16), projected], axis=0)
    rims = padded[:group_rows].reshape(tp_count, dev_rows, total_cols)[:, :rim_rows]
    blocks = jnp.concatenate([rims, projected.reshape(tp_count, dev_rows, total_cols)], axis=1)
    arrived = lax.all_to_all(blocks, "tp", split_axis=0, concat_axis=2, tiled=True).reshape(
        dev_rows + rim_rows, tp_count, total_cols
    )

    def columns(source, which):
        return source[:, :, col_edges[which] : col_edges[which + 1]].reshape(source.shape[0], -1)

    gate_in = columns(arrived[rim_rows:], 0).astype(jnp.float32)
    conv_in = jnp.concatenate(
        [columns(arrived, 1), columns(arrived, 2), columns(arrived, 3)], axis=1
    ).astype(jnp.float32)
    dt_in = columns(arrived[rim_rows:], 4).astype(jnp.float32)

    def prepare(conv_in, dt_in, conv_w, conv_b, dt_bias, a_log):
        summed = jnp.zeros((dev_rows, conv_in.shape[1]), jnp.float32) + conv_b[None, :]
        for kernel_tap in range(conv_w.shape[1]):
            match = (seg_ext[kernel_tap : kernel_tap + dev_rows] == seg_own).astype(jnp.float32)
            summed = (
                summed
                + conv_w[:, kernel_tap][None, :]
                * conv_in[kernel_tap : kernel_tap + dev_rows]
                * match[:, None]
            )
        active = jax.nn.silu(summed)
        values = active[:, :inner_width].reshape(dev_rows, head_count, head_size)
        b_rows = active[:, inner_width : inner_width + state_size]
        c_rows = active[:, inner_width + state_size :]
        steps_dt = jax.nn.softplus(dt_in + dt_bias[None, :])
        log_decay = -steps_dt * jnp.exp(a_log)[None, :]
        return (values, b_rows, c_rows, log_decay, steps_dt)

    prepared, prepare_back = jax.vjp(prepare, conv_in, dt_in, conv_w, conv_b, dt_bias, a_log)
    values, b_rows, c_rows, log_decay, steps_dt = prepared

    def ssd_local(values, b_rows, c_rows, log_decay, steps_dt):
        state = jnp.zeros((head_count, head_size, state_size), jnp.float32)
        carried_all = jnp.ones((head_count,), jnp.float32)
        output, state, carried = span_pass(
            state, values, b_rows, c_rows, log_decay, steps_dt, seg_own, seg_before[0]
        )
        outputs = [output]
        carried_all = carried_all * carried
        return (jnp.concatenate(outputs, axis=0), carried_all, state)

    def entering(state_in, c_rows, log_decay):
        decay = jnp.ones((head_count,), jnp.float32)
        cumulative, inward, carried = span_parts(log_decay, seg_own, seg_before[0])
        reached = jnp.einsum(
            "tn,hpn->thp", c_rows, decay[:, None, None] * state_in, precision=HIGHEST
        )
        outputs = [reached * inward[:, :, None]]
        return jnp.concatenate(outputs, axis=0)

    identity = (
        jnp.ones((head_count,), jnp.float32),
        jnp.zeros((head_count, head_size, state_size), jnp.float32),
    )
    local_parts, ssd_back = jax.vjp(ssd_local, values, b_rows, c_rows, log_decay, steps_dt)
    local_out, carried_dev, state_dev = local_parts
    chained = entering_2((carried_dev, state_dev), "tp", combine, identity, False)
    state_in = chained[1]
    extra_out, entering_back = jax.vjp(entering, state_in, c_rows, log_decay)
    ssd_out = local_out + extra_out

    def gated(ssd_out, values, gate_in, d_skip, gate_gain):
        mixed_heads = ssd_out + d_skip[None, :, None] * values
        flat = mixed_heads.reshape(dev_rows, inner_width)
        gated_rows = flat * jax.nn.silu(gate_in)
        scale = lax.rsqrt(jnp.mean(gated_rows * gated_rows, axis=-1, keepdims=True) + EPSILON)
        return gated_rows * scale * gate_gain[None, :]

    normal_out, gated_back = jax.vjp(gated, ssd_out, values, gate_in, d_skip, gate_gain)
    rounded = normal_out.astype(jnp.bfloat16)
    by_heads = lax.all_to_all(rounded, "tp", split_axis=1, concat_axis=0, tiled=True)
    branch_out = lax.psum_scatter(
        jnp.dot(by_heads, w_out, preferred_element_type=jnp.float32),
        "tp",
        scatter_dimension=0,
        tiled=True,
    )
    block_out = (x_float + branch_out).astype(jnp.bfloat16)
    grad_gathered = lax.all_gather(d_out, "tp", axis=0, tiled=True)
    grad_heads = lax.dot_general(
        grad_gathered, w_out, contract_last, preferred_element_type=jnp.float32
    ).astype(jnp.bfloat16)
    grad_normal = lax.all_to_all(grad_heads, "tp", split_axis=0, concat_axis=1, tiled=True)
    grad_ssd, grad_values_a, grad_gate_in, grad_skip, grad_gate_gain = gated_back(
        grad_normal.astype(jnp.float32)
    )
    grad_state_in, grad_c_a, grad_decay_a = entering_back(grad_ssd)
    chained_back = entering_2((carried_dev, grad_state_in), "tp", combine, identity, True)
    grad_state_dev = chained_back[1]
    grad_carried = jnp.sum(grad_state_dev * state_in, axis=(1, 2))
    grad_values_b, grad_b, grad_c_b, grad_decay_b, grad_dt = ssd_back(
        (grad_ssd, grad_carried, grad_state_dev)
    )
    grad_conv_in, grad_dt_in, grad_conv_w, grad_conv_b, grad_dt_bias, grad_a_log = prepare_back(
        (
            grad_values_a + grad_values_b,
            grad_b,
            grad_c_a + grad_c_b,
            grad_decay_a + grad_decay_b,
            grad_dt,
        )
    )

    def split_heads(array):
        return array.reshape(array.shape[0], tp_count, -1)

    grad_gate_full = jnp.concatenate(
        [jnp.zeros((rim_rows, inner_width), jnp.float32), grad_gate_in], axis=0
    )
    grad_dt_full = jnp.concatenate(
        [jnp.zeros((rim_rows, head_count), jnp.float32), grad_dt_in], axis=0
    )
    pieces = [
        split_heads(grad_gate_full),
        split_heads(grad_conv_in[:, :inner_width]),
        split_heads(grad_conv_in[:, inner_width : inner_width + state_size]),
        split_heads(grad_conv_in[:, inner_width + state_size :]),
        split_heads(grad_dt_full),
    ]
    outgoing = jnp.concatenate(pieces, axis=2).reshape(
        1, dev_rows + rim_rows, tp_count * total_cols
    )
    returned = lax.all_to_all(outgoing, "tp", split_axis=2, concat_axis=0, tiled=True)
    main_rows = returned[:, rim_rows:]
    main_rows = main_rows.at[:-1, dev_rows - rim_rows :].add(returned[1:, :rim_rows])
    grad_projected = main_rows.reshape(group_rows, total_cols).astype(jnp.bfloat16)
    grad_normed = lax.psum_scatter(
        lax.dot_general(
            grad_projected, w_joined, contract_last, preferred_element_type=jnp.float32
        ),
        "tp",
        scatter_dimension=0,
        tiled=True,
    )
    _, norm_back = jax.vjp(in_norm, x_float, norm_gain)
    grad_x_norm, grad_norm_gain = norm_back(grad_normed)
    grad_x = d_out.astype(jnp.float32) + grad_x_norm
    in_part = lax.dot_general(
        gathered, grad_projected, contract_first, preferred_element_type=jnp.float32
    )
    weight_grads = lax.psum_scatter(
        jnp.concatenate(
            [
                in_part,
                lax.dot_general(
                    grad_gathered, by_heads, contract_first, preferred_element_type=jnp.float32
                ),
            ],
            axis=1,
        ),
        "dp",
        scatter_dimension=0,
        tiled=True,
    )
    grad_w_z = weight_grads[:, col_edges[0] : col_edges[1]]
    grad_w_x = weight_grads[:, col_edges[1] : col_edges[2]]
    grad_w_b = weight_grads[:, col_edges[2] : col_edges[3]]
    grad_w_c = weight_grads[:, col_edges[3] : col_edges[4]]
    grad_w_dt = weight_grads[:, col_edges[4] : col_edges[5]]
    grad_w_out = weight_grads[:, total_cols:].T
    summed_small = lax.psum(
        (
            grad_norm_gain,
            grad_conv_w,
            grad_conv_b,
            grad_dt_bias,
            grad_a_log,
            grad_skip,
            grad_gate_gain,
        ),
        ("dp", "tp"),
    )
    return (
        block_out,
        grad_x,
        summed_small[0],
        grad_w_z,
        grad_w_x,
        grad_w_b,
        grad_w_c,
        grad_w_dt,
        summed_small[1],
        summed_small[2],
        summed_small[3],
        summed_small[4],
        summed_small[5],
        summed_small[6],
        grad_w_out,
    )


def solution(mesh):
    placed = (
        P(("dp", "tp"), None),
        P(),
        P(None, "tp"),
        P(None, "tp"),
        P(None, "tp"),
        P(None, "tp"),
        P(None, "tp"),
        P(),
        P(),
        P(),
        P(),
        P(),
        P(),
        P("tp", None),
        P("dp", None),
        P(("dp", "tp"), None),
    )
    return jax.shard_map(
        body,
        mesh=mesh,
        in_specs=placed,
        out_specs=(
            P(("dp", "tp"), None),
            P(("dp", "tp"), None),
            P(),
            P("dp", "tp"),
            P("dp", "tp"),
            P("dp", "tp"),
            P("dp", "tp"),
            P("dp", "tp"),
            P(),
            P(),
            P(),
            P(),
            P(),
            P(),
            P("tp", "dp"),
        ),
        check_vma=False,
    )
```

profile of v0, /device:TPU:1, one launch (start us, length us, event | category | flops | bytes accessed | tf_op | source)
XLA Modules:
  0.0 1443.4 jit_solution(17318158812077434221)
XLA Ops:
  12.3 14.3 concatenate.29
  26.6 39.8 %all-gather.8.cloned.1.call-done = bf16[1024,2048]{1,0:T(8,128)(2,1)} async-done(((bf16[256,2048]{1,0:T(8,128)(2,1)}), bf16[1024,2048]{1,0:T(8,128)(2,1)}) %all-gather.8.cloned.1.call-update) | async-done | bytes 4194320 | tf_op jit(solution)/shard_map/all_gather | solution.py:115
  66.3 13.6 convolution_convert_fusion
  86.6 6.4 copy.204
  93.1 6.4 copy.203
  117.4 60.6 %all-to-all-done = bf16[4,259,2128]{2,1,0:T(8,128)(2,1)} async-done(((bf16[4,259,2128]{2,1,0:T(8,128)(2,1)}), bf16[4,259,2128]{2,1,0:T(8,128)(2,1)}, u32[]{:S(2)}, u32[]{:S(2)}) %all-to-all-start) | async-done | bytes 4409248 | tf_op jit(solution)/shard_map/all_to_all | solution.py:120
  178.0 8.2 copy.176
  218.3 7.0 fusion.78
  225.4 8.0 convolution_convert_fusion.1
  240.8 43.3 %all-to-all-done.2 = bf16[4,256,1024]{1,2,0:T(8,128)(2,1)} async-done(((bf16[4,256,1024]{1,2,0:T(8,128)(2,1)}), bf16[4,256,1024]{1,2,0:T(8,128)(2,1)}, u32[]{:S(2)}, u32[]{:S(2)}) %all-to-all-start.2) | async-done | bytes 2097184 | tf_op jit(solution)/shard_map/all_to_all | solution.py:205
  288.1 6.3 all-gather.2
  295.7 6.2 fusion.92
  305.8 32.7 %all-gather.12.cloned.1.call-done = f32[256,64,128]{2,1,0:T(8,128)} async-done(((f32[64,64,128]{2,1,0:T(8,128)}), f32[256,64,128]{2,1,0:T(8,128)}) %all-gather.12.cloned.1.call-update) | async-done | bytes 8388624 | tf_op jit(solution)/shard_map/all_gather | solution.py:12
  338.5 8.5 while.31
  351.5 23.6 %multiply_reduce_fusion.11 = (f32[256]{0:T(256)S(1)}, f32[256,64,64]{0,2,1:T(8,128)S(1)}, f32[256,64,64]{0,2,1:T(8,128)}) fusion(f32[256,64,64]{0,2,1:T(8,128)} %bitcast.311, f32[256,64,64]{0,2,1:T(8,128)S(1)} %bitcast.299, f32[64]{0:T(128)S(1)} %copy-done.73, f32[256,64,64]{0,2,1:T(8,128)S(1)} %fusion.100, f32[256,64,64]{0,2,1:T(8,128)} %fusion.92, ...), kind=kOutput, calls=%fused_computation.87 | convolution fusion | flops 3251633920 | bytes 25691392 | tf_op jit(solution)/shard_map/jvp(tsh,shp->thp)/dot_general | solution.py:44
  377.4 6.0 multiply_reduce_fusion.6
  403.4 7.6 copy.193
  411.0 8.8 fusion.84
  419.8 6.7 fusion.81
  426.6 26.2 %fusion.10 = (f32[256,64]{0,1:T(8,128)S(1)}, f32[256,64]{0,1:T(8,128)S(1)}, f32[256,64]{0,1:T(8,128)}, f32[256,256]{1,0:T(8,128)S(1)}) fusion(f32[256,64]{0,1:T(8,128)S(1)} %copy-done.43, f32[256,256]{1,0:T(8,128)S(1)} %copy-done.23, f32[256,64]{0,1:T(8,128)S(1)} %bitcast_bitcast_fusion.1, pred[256,256]{1,0:T(8,128)(4,1)S(1)} %fusion.95, ...), kind=kOutput, calls=%fused_computation.18 | convolution fusion | flops 3275636736 | bytes 9306112 | tf_op jit(solution)/shard_map/transpose(jvp(tsh,shp->thp))/dot_general | solution.py:44
  454.0 24.7 %all-gather.14.cloned.1.call-done = f32[256,64,128]{2,1,0:T(8,128)} async-done(((f32[64,64,128]{2,1,0:T(8,128)}), f32[256,64,128]{2,1,0:T(8,128)}) %all-gather.14.cloned.1.call-update) | async-done | bytes 8388624 | tf_op jit(solution)/shard_map/all_gather | solution.py:12
  478.7 14.9 %while.32 = (s32[]{:T(128)}, f32[64,64,128]{2,1,0:T(8,128)}, s32[]{:T(128)}, f32[4,64]{1,0:T(4,128)S(1)}, f32[4,64,64,128]{3,2,1,0:T(8,128)}, /*index=5*/s32[]{:T(128)}, s32[]{:T(128)}, s32[]{:T(128)}, s32[]{:T(128)}) while((s32[]{:T(128)}, f32[64,64,128]{2,1,0:T(8,128)}, s32[]{:T(128)}, f32[4,64]{1,0:T(4,128)S(1)}, ...), condition=%wide.region_12.13_spmd.clone, body=%wide.region_11.12_spmd.clone.sunk | while | flops 2097160 | bytes 6292391 | solution.py:25
  493.6 9.8 fusion.87
  510.5 15.7 %fusion.31 = f32[256,64,64]{0,2,1:T(8,128)} fusion(f32[256,64,64]{0,2,1:T(8,128)S(1)} %get-tuple-element.469, f32[256,64,64]{0,2,1:T(8,128)S(1)} %copy-done.7, f32[64]{0:T(128)S(1)} %copy-done.73, f32[256,64]{0,1:T(8,128)S(1)} %get-tuple-element.456, f32[256,64]{0,1:T(8,128)S(1)} %copy-done.43, f32[256,256]{1,0:T(8,128)S(1)} %copy-done.24, ...), kind=kOutput, calls=%fused_computation.58 | convolution fusion | flops 3242196992 | bytes 13107456 | tf_op jit(solution)/shard_map/transpose(jvp(tsh,shp->thp))/dot_general | solution.py:44
  526.2 6.0 copy.185
  532.2 12.2 multiply_reduce_fusion.4
  549.5 7.2 pad_add_fusion
  566.3 6.1 reshape.445
  572.4 15.8 %concatenate.35 = f32[259,4,2128]{2,1,0:T(4,128)} concatenate(f32[259,4,1024]{2,1,0:T(4,128)} %copy.193, f32[259,4,1024]{2,1,0:T(4,128)} %reshape.445, f32[259,4,32]{2,1,0:T(4,128)S(1)} %copy.194, f32[259,4,32]{2,1,0:T(4,128)S(1)} %copy.195, f32[259,4,16]{2,1,0:T(4,128)S(1)} %copy.196), dimensions={2} | concatenate | bytes 17636864 | tf_op jit(solution)/shard_map/concatenate | solution.py:242
  588.2 11.4 reshape.454
  599.6 27.3 %copy.197 = f32[1,259,8512]{1,0,2:T(1,128)} copy(f32[1,259,8512]{2,1,0:T(8,128)} %reshape.454) | data formatting | bytes 17636864 | tf_op jit(solution)/shard_map/reshape | solution.py:242
  626.8 6.5 all-to-all-start.3
  634.7 140.7 %all-to-all-done.3 = f32[1,259,8512]{1,0,2:T(1,128)} async-done(((f32[1,259,8512]{1,0,2:T(1,128)}), f32[1,259,8512]{1,0,2:T(1,128)}, u32[]{:S(2)}, u32[]{:S(2)}) %all-to-all-start.3) | async-done | bytes 8818464 | tf_op jit(solution)/shard_map/all_to_all | solution.py:245
  775.4 11.9 copy.207
  787.3 7.0 slice.233
  802.5 22.9 %scatter-add.4 = f32[4,256,2128]{1,2,0:T(8,128)} dynamic-update-slice(f32[4,256,2128]{1,2,0:T(8,128)} %copy-done.8, f32[3,3,2128]{1,2,0:T(8,128)S(1)} %add_select_fusion, s32[]{:T(128)} %bitcast.52, s32[]{:T(128)} %bitcast.53, s32[]{:T(128)} %constant.140.clone.1) | dynamic-update-slice | bytes 153220 | tf_op jit(solution)/shard_map/scatter-add | solution.py:247
  825.4 5.9 convert_element_type.125
  831.3 6.4 copy.200
  837.7 15.7 %fusion.148 = f32[1024,2048]{1,0:T(8,128)} fusion(bf16[1024,2128]{1,0:T(8,128)(2,1)} %bitcast.319, bf16[2048,2128]{1,0:T(8,128)(2,1)} %concatenate.29), kind=kOutput, calls=%fused_computation.237 | convolution fusion | flops 8925478912 | bytes 21463040 | tf_op jit(solution)/shard_map/dot_general | solution.py:250
  857.8 49.7 %all_to_all.62 = bf16[256,4,1024]{0,2,1:T(8,128)(2,1)S(1)} all-to-all(bf16[256,4,1024]{0,2,1:T(8,128)(2,1)S(1)} %fusion.48), channel_id=1, replica_groups=mesh['dp'=8,'tp'=4] {'tp'}, dimensions={1} | all-to-all | bytes 4194304 | tf_op jit(solution)/shard_map/all_to_all | solution.py:193
  909.9 10.7 fusion.147
  922.2 9.1 convolution_bitcast_fusion
  931.3 12.9 fusion.149
  944.2 16.0 %pad_maximum_fusion = f32[2048,3152]{0,1:T(8,128)} fusion(f32[2048,1024]{0,1:T(8,128)} %convolution_bitcast_fusion, f32[2048,2128]{0,1:T(8,128)S(1)} %fusion.149), kind=kLoop, calls=%fused_computation.6 | loop fusion | flops 6455296 | bytes 51642368 | tf_op jit(solution)/shard_map/concatenate | solution.py:264
  965.7 41.9 %all-reduce.16 = (f32[2048]{0:T(1024)}, f32[4352]{0:T(1024)}, f32[64]{0:T(128)}, f32[64]{0:T(128)}, f32[64]{0:T(128)}, /*index=5*/f32[4096]{0:T(1024)}) all-reduce(f32[2048]{0:T(1024)S(1)} %get-tuple-element.395, f32[4352]{0:T(1024)S(1)} %copy-done.32, f32[64]{0:T(128)S(1)} %get-tuple-element.431, ...), channel_id=1, replica_groups=mesh['dp'=8,'tp'=4] {'dp','tp'}, use_global_device_ids=true, to_apply=%region_30.31 | all-reduce | flops 10688 | bytes 85504 | tf_op jit(solution)/shard_map/psum | solution.py:283
  1007.6 46.4 %reduce-scatter.4.cloned.1.call-done = f32[256,2048]{1,0:T(8,128)} async-done(((f32[1024,2048]{1,0:T(8,128)}), f32[256,2048]{1,0:T(8,128)}) %reduce-scatter.4.cloned.1.call-update) | async-done | bytes 2097168 | tf_op jit(solution)/shard_map/reduce_scatter | solution.py:194
  1058.3 249.3 %reduce-scatter.8.cloned.1.call-done = f32[256,3152]{0,1:T(8,128)} async-done(((f32[2048,3152]{0,1:T(8,128)}), f32[256,3152]{0,1:T(8,128)}) %reduce-scatter.8.cloned.1.call-update) | async-done | bytes 3227664 | tf_op jit(solution)/shard_map/reduce_scatter | solution.py:263
  1316.0 118.6 %all-reduce.19.cloned.1.call-done = f32[4352,4]{0,1:T(4,128)} async-done(((f32[4352,4]{0,1:T(4,128)}), f32[4352,4]{0,1:T(4,128)}) %all-reduce.19.cloned.1.call-update) | async-done | bytes 69648 | tf_op jit(solution)/shard_map/psum | solution.py:283
  (293 shorter events, 186.9 us)
Async XLA Ops:
  7.2 59.1 %all-gather.8.cloned.1.call-start = ((), (), s32[]{:S(2)}) async-start(), calls=%async_computation.7 | async-start | bytes 5242880 | tf_op jit(solution)/shard_map/all_gather | solution.py:115
  106.0 6.4 copy-start.74
  106.0 6.4 copy-start.72
  106.0 8.6 copy-start.38
  106.0 72.0 %all-to-all-start = ((bf16[4,259,2128]{2,1,0:T(8,128)(2,1)}), bf16[4,259,2128]{2,1,0:T(8,128)(2,1)}, u32[]{:S(2)}, u32[]{:S(2)}) async-start(bf16[4,259,2128]{2,1,0:T(8,128)(2,1)} %pad_maximum_fusion.1), calls=%async_computation | async-start | bytes 9191424 | tf_op jit(solution)/shard_map/all_to_all | solution.py:120
  111.1 114.3 %all-gather.10.cloned.1.call-start = ((), (), s32[]{:S(2)}) async-start(), calls=%async_computation.9 | async-start | bytes 5242880 | tf_op jit(solution)/shard_map/all_gather | solution.py:201
  111.8 226.7 %all-gather.12.cloned.1.call-start = ((), (), s32[]{:S(2)}) async-start(), calls=%async_computation.13 | async-start | bytes 10485760 | tf_op jit(solution)/shard_map/all_gather | solution.py:12
  112.4 80.9 %copy-start.68 = (f32[64]{0:T(128)}, f32[64]{0:T(128)S(1)}, u32[]{:S(2)}) copy-start(f32[64]{0:T(128)S(1)} %exp.58) | copy-start | bytes 772
  112.7 73.5 %copy-start.45 = (s32[259]{0:T(512)}, s32[259]{0:T(512)S(1)}, u32[]{:S(2)}) copy-start(s32[259]{0:T(512)S(1)} %convert_reduce_fusion) | copy-start | bytes 3112
  186.2 7.2 copy-start.59
  193.4 24.8 %copy-start.20 = (bf16[256,4,16]{0,2,1:T(8,128)(2,1)}, bf16[256,4,16]{0,2,1:T(8,128)(2,1)S(1)}, u32[]{:S(2)}) copy-start(bf16[256,4,16]{0,2,1:T(8,128)(2,1)S(1)} %slice.224) | copy-start | bytes 98308
  212.0 6.1 copy-start.50
  212.0 6.1 copy-start.60
  212.0 6.1 copy-start.64
  218.1 7.2 copy-start.62
  218.3 133.2 %copy-start.42 = (f32[256,64]{0,1:T(8,128)}, f32[256,64]{0,1:T(8,128)S(1)}, u32[]{:S(2)}) copy-start(f32[256,64]{0,1:T(8,128)S(1)} %get-tuple-element.457) | copy-start | bytes 196612
  233.4 7.2 copy-start.46
  233.4 7.2 copy-start.27
  236.0 48.2 %all-to-all-start.2 = ((bf16[4,256,1024]{1,2,0:T(8,128)(2,1)}), bf16[4,256,1024]{1,2,0:T(8,128)(2,1)}, u32[]{:S(2)}, u32[]{:S(2)}) async-start(bf16[4,256,1024]{1,2,0:T(8,128)(2,1)} %copy.184), calls=%async_computation.3 | async-start | bytes 4194304 | tf_op jit(solution)/shard_map/all_to_all | solution.py:205
  240.5 238.3 %all-gather.14.cloned.1.call-start = ((), (), s32[]{:S(2)}) async-start(), calls=%async_computation.14 | async-start | bytes 10485760 | tf_op jit(solution)/shard_map/all_gather | solution.py:12
  240.8 185.7 %copy-start.40 = (pred[256,256]{1,0:T(8,128)(4,1)}, pred[256,256]{1,0:T(8,128)(4,1)S(1)}, u32[]{:S(2)}) copy-start(pred[256,256]{1,0:T(8,128)(4,1)S(1)} %fusion.95) | copy-start | bytes 196612
  295.7 55.8 %copy-start.22 = (f32[256,256]{1,0:T(8,128)}, f32[256,256]{1,0:T(8,128)S(1)}, u32[]{:S(2)}) copy-start(f32[256,256]{1,0:T(8,128)S(1)} %fusion.106) | copy-start | bytes 786436
  351.5 23.7 %copy-start.16 = (f32[256,64,64]{0,2,1:T(8,128)}, f32[256,64,64]{0,2,1:T(8,128)S(1)}, u32[]{:S(2)}) copy-start(f32[256,64,64]{0,2,1:T(8,128)S(1)} %fusion.100) | copy-start | bytes 12582916
  351.5 23.6 %copy-start.11 = (f32[4,256,1024]{1,2,0:T(8,128)S(1)}, f32[4,256,1024]{1,2,0:T(8,128)}, u32[]{:S(2)}) copy-start(f32[4,256,1024]{1,2,0:T(8,128)} %convert_element_type.132) | copy-start | bytes 12582916
  375.1 18.6 %copy-start.47 = (f32[256]{0:T(256)}, f32[256]{0:T(256)S(1)}, u32[]{:S(2)}) copy-start(f32[256]{0:T(256)S(1)} %fusion.132) | copy-start | bytes 3076
  411.0 8.8 copy-start.6
  419.8 6.7 copy-start.3
  419.8 6.7 copy-start.23
  419.8 6.7 copy-start.43
  493.6 9.9 copy-start.1
  493.6 9.9 copy-start.4
  526.2 6.0 copy-start.52
  526.2 6.0 copy-start.54
  526.2 6.0 copy-start.56
  549.4 7.2 copy-start.21
  549.4 7.2 copy-start.61
  549.4 7.2 copy-start.63
  549.4 7.2 copy-start.65
  549.4 10.6 copy-start.44
  549.5 10.6 copy-start.69
  626.8 7.1 copy-start.71
  626.8 148.5 %all-to-all-start.3 = ((f32[1,259,8512]{1,0,2:T(1,128)}), f32[1,259,8512]{1,0,2:T(1,128)}, u32[]{:S(2)}, u32[]{:S(2)}) async-start(f32[1,259,8512]{1,0,2:T(1,128)} %copy.197), calls=%async_computation.4 | async-start | bytes 26148864 | tf_op jit(solution)/shard_map/all_to_all | solution.py:245
  633.3 329.9 %reduce-scatter.6.cloned.1.call-start = ((), (), s32[]{:S(2)}) async-start(), calls=%async_computation.10 | async-start | bytes 10485760 | tf_op jit(solution)/shard_map/reduce_scatter | solution.py:249
  853.5 200.5 %reduce-scatter.4.cloned.1.call-start = ((), (), s32[]{:S(2)}) async-start(), calls=%async_computation.8 | async-start | bytes 10485760 | tf_op jit(solution)/shard_map/reduce_scatter | solution.py:194
  920.6 387.0 %reduce-scatter.8.cloned.1.call-start = ((), (), s32[]{:S(2)}) async-start(), calls=%async_computation.11 | async-start | bytes 29048832 | tf_op jit(solution)/shard_map/reduce_scatter | solution.py:263
  960.3 5.4 copy-start.32
  960.3 474.2 %all-reduce.19.cloned.1.call-start = ((), (), s32[]{:S(2)}) async-start(), calls=%async_computation.12 | async-start | bytes 139264 | tf_op jit(solution)/shard_map/psum | solution.py:283
  963.3 90.7 %copy-start.18 = (f32[256,2048]{1,0:T(8,128)S(1)}, f32[256,2048]{1,0:T(8,128)}, u32[]{:S(2)}) copy-start(f32[256,2048]{1,0:T(8,128)} %reduce-scatter.6.cloned.1.call-done) | copy-start | bytes 6291460
  (39 other events, 99.8 us)
Sparse Core Ops, SparseCore 0:
  11.5 54.7 all-gather.7
  113.7 83.3 all-gather.9
  225.4 113.0 all-gather.11
  391.1 87.6 all-gather.13
  853.6 109.6 reduce-scatter.5
  966.5 87.4 reduce-scatter.3
  1056.3 251.1 reduce-scatter.7
  1314.7 119.8 all-reduce.18
where the time goes:
time: 1460 us; the launch traced here: 1440 us
  waiting for transfers between devices  758 us (52%)
  local copies, waits for them, and re-layouts  230 us (16%)
  matrix products  193 us (13%)
  other arithmetic  130 us (9%)
  blocking collectives  97.8 us (7%)
  between operations  17.1 us (1%)
  starting transfers between devices  16.9 us (1%)
    reduce_scatter x1, waiting for transfers between devices, body(): lax.psum_scatter(jnp.concatenate([in_part, lax.dot_general(grad_gathered,...  249 us
    all_to_all x1, waiting for transfers between devices, body(): lax.all_to_all(outgoing, 'tp', split_axis=2, concat_axis=0, tiled=True)  141 us
    psum x1, waiting for transfers between devices, body(): lax.psum((grad_norm_gain, grad_conv_w, grad_conv_b, grad_dt_bias, grad_a_...  119 us
    dot_general x3, matrix products, span_pass(): output = jnp.einsum('tsh,shp->thp', mixing, values, precision=HIGHEST)  65.4 us
    all_to_all x1, waiting for transfers between devices, body(): lax.all_to_all(blocks, 'tp', split_axis=0, concat_axis=2, tiled=True)  60.6 us
    all_gather x2, waiting for transfers between devices, entering_2(): everything = jax.tree.map(lambda part: lax.all_gather(part, axis), array)  57.4 us
    all_to_all x1, blocking collectives, body(): lax.all_to_all(rounded, 'tp', split_axis=1, concat_axis=0, tiled=True)  49.7 us
    reduce_scatter x1, waiting for transfers between devices, body(): lax.psum_scatter(jnp.dot(by_heads, w_out, preferred_element_type=jnp.floa...  46.4 us
  transfers between devices with their start and end apart: 11, of which 10 were waited for; matrix products, arithmetic and copies ran while one was open for 15% of the time, Pallas kernels for 0%

commit v1 on v0

--- a/solution.py
+++ b/solution.py
@@ -117,9 +117,10 @@
     padded = jnp.concatenate([jnp.zeros((rim_rows, total_cols), jnp.bfloat16), projected], axis=0)
     rims = padded[:group_rows].reshape(tp_count, dev_rows, total_cols)[:, :rim_rows]
     blocks = jnp.concatenate([rims, projected.reshape(tp_count, dev_rows, total_cols)], axis=1)
-    arrived = lax.all_to_all(blocks, "tp", split_axis=0, concat_axis=2, tiled=True).reshape(
-        dev_rows + rim_rows, tp_count, total_cols
-    )
+    arrived = jnp.concatenate(
+        lax.all_to_all(jnp.stack(jnp.split(blocks, lax.axis_size("tp"), axis=0)), "tp", 0, 0),
+        axis=2,
+    ).reshape(dev_rows + rim_rows, tp_count, total_cols)
 
     def columns(source, which):
         return source[:, :, col_edges[which] : col_edges[which + 1]].reshape(source.shape[0], -1)

time: 1460 us -> 1460 us (level)
  no operation moved by 1% of the time
where the time goes in v1:
time: 1460 us; the launch traced here: 1440 us
  waiting for transfers between devices  758 us (52%)
  local copies, waits for them, and re-layouts  230 us (16%)
  matrix products  193 us (13%)
  other arithmetic  131 us (9%)
  blocking collectives  97.8 us (7%)
  between operations  17.1 us (1%)
  starting transfers between devices  16.9 us (1%)
    reduce_scatter x1, waiting for transfers between devices, body(): lax.psum_scatter(jnp.concatenate([in_part, lax.dot_general(grad_gathered,...  249 us
    all_to_all x1, waiting for transfers between devices, body(): lax.all_to_all(outgoing, 'tp', split_axis=2, concat_axis=0, tiled=True)  141 us
    psum x1, waiting for transfers between devices, body(): lax.psum((grad_norm_gain, grad_conv_w, grad_conv_b, grad_dt_bias, grad_a_...  119 us
    dot_general x3, matrix products, span_pass(): output = jnp.einsum('tsh,shp->thp', mixing, values, precision=HIGHEST)  65.4 us
    all_to_all x1, waiting for transfers between devices, body(): lax.all_to_all(jnp.stack(jnp.split(blocks, lax.axis_size('tp'), axis=0)),...  60.6 us
    all_gather x2, waiting for transfers between devices, entering_2(): everything = jax.tree.map(lambda part: lax.all_gather(part, axis), array)  57.4 us
    all_to_all x1, blocking collectives, body(): lax.all_to_all(rounded, 'tp', split_axis=1, concat_axis=0, tiled=True)  49.7 us
    reduce_scatter x1, waiting for transfers between devices, body(): lax.psum_scatter(jnp.dot(by_heads, w_out, preferred_element_type=jnp.floa...  46.4 us
  transfers between devices with their start and end apart: 11, of which 10 were waited for; matrix products, arithmetic and copies ran while one was open for 15% of the time, Pallas kernels for 0%

profile of v1, /device:TPU:1, one launch (start us, length us, event | category | flops | bytes accessed | tf_op | source)
XLA Modules:
  0.0 1444.1 jit_solution(8761543569129856060)
XLA Ops:
  12.3 14.3 concatenate.29
  26.6 39.8 %all-gather.8.cloned.1.call-done = bf16[1024,2048]{1,0:T(8,128)(2,1)} async-done(((bf16[256,2048]{1,0:T(8,128)(2,1)}), bf16[1024,2048]{1,0:T(8,128)(2,1)}) %all-gather.8.cloned.1.call-update) | async-done | bytes 4194320 | tf_op jit(solution)/shard_map/all_gather | solution.py:115
  66.3 13.6 convolution_convert_fusion
  86.6 6.4 copy.264
  93.1 6.4 copy.263
  118.1 60.6 %all-to-all-done = bf16[4,1,259,2128]{3,2,1,0:T(8,128)(2,1)} async-done(((bf16[4,1,259,2128]{3,2,1,0:T(8,128)(2,1)}), bf16[4,1,259,2128]{3,2,1,0:T(8,128)(2,1)}, u32[]{:S(2)}, u32[]{:S(2)}) %all-to-all-start) | async-done | bytes 4409248 | tf_op jit(solution)/shard_map/all_to_all | solution.py:121
  178.7 8.2 copy.265
  219.1 7.0 fusion.78
  226.1 8.0 convolution_convert_fusion.1
  241.5 43.3 %all-to-all-done.2 = bf16[4,256,1024]{1,2,0:T(8,128)(2,1)} async-done(((bf16[4,256,1024]{1,2,0:T(8,128)(2,1)}), bf16[4,256,1024]{1,2,0:T(8,128)(2,1)}, u32[]{:S(2)}, u32[]{:S(2)}) %all-to-all-start.2) | async-done | bytes 2097184 | tf_op jit(solution)/shard_map/all_to_all | solution.py:206
  288.8 6.3 all-gather.2
  296.4 6.2 fusion.99
  306.5 32.7 %all-gather.12.cloned.1.call-done = f32[256,64,128]{2,1,0:T(8,128)} async-done(((f32[64,64,128]{2,1,0:T(8,128)}), f32[256,64,128]{2,1,0:T(8,128)}) %all-gather.12.cloned.1.call-update) | async-done | bytes 8388624 | tf_op jit(solution)/shard_map/all_gather | solution.py:12
  339.2 8.5 while.31
  352.3 23.6 %multiply_reduce_fusion.11 = (f32[256]{0:T(256)S(1)}, f32[256,64,64]{0,2,1:T(8,128)S(1)}, f32[256,64,64]{0,2,1:T(8,128)}) fusion(f32[256,64,64]{0,2,1:T(8,128)} %bitcast.317, f32[256,64,64]{0,2,1:T(8,128)S(1)} %bitcast.305, f32[64]{0:T(128)S(1)} %copy-done.73, f32[256,64,64]{0,2,1:T(8,128)S(1)} %fusion.107, f32[256,64,64]{0,2,1:T(8,128)} %fusion.99, ...), kind=kOutput, calls=%fused_computation.90 | convolution fusion | flops 3251633920 | bytes 25691392 | tf_op jit(solution)/shard_map/jvp(tsh,shp->thp)/dot_general | solution.py:44
  378.1 6.0 multiply_reduce_fusion.6
  404.1 7.6 copy.282
  411.7 8.8 fusion.91
  420.6 6.7 fusion.88
  427.3 26.2 %fusion.10 = (f32[256,64]{0,1:T(8,128)S(1)}, f32[256,64]{0,1:T(8,128)S(1)}, f32[256,64]{0,1:T(8,128)}, f32[256,256]{1,0:T(8,128)S(1)}) fusion(f32[256,64]{0,1:T(8,128)S(1)} %copy-done.43, f32[256,256]{1,0:T(8,128)S(1)} %copy-done.23, f32[256,64]{0,1:T(8,128)S(1)} %bitcast_bitcast_fusion.1, pred[256,256]{1,0:T(8,128)(4,1)S(1)} %fusion.102, ...), kind=kOutput, calls=%fused_computation.18 | convolution fusion | flops 3275636736 | bytes 9306112 | tf_op jit(solution)/shard_map/transpose(jvp(tsh,shp->thp))/dot_general | solution.py:44
  454.7 24.7 %all-gather.14.cloned.1.call-done = f32[256,64,128]{2,1,0:T(8,128)} async-done(((f32[64,64,128]{2,1,0:T(8,128)}), f32[256,64,128]{2,1,0:T(8,128)}) %all-gather.14.cloned.1.call-update) | async-done | bytes 8388624 | tf_op jit(solution)/shard_map/all_gather | solution.py:12
  479.5 14.9 %while.32 = (s32[]{:T(128)}, f32[64,64,128]{2,1,0:T(8,128)}, s32[]{:T(128)}, f32[4,64]{1,0:T(4,128)S(1)}, f32[4,64,64,128]{3,2,1,0:T(8,128)}, /*index=5*/s32[]{:T(128)}, s32[]{:T(128)}, s32[]{:T(128)}, s32[]{:T(128)}) while((s32[]{:T(128)}, f32[64,64,128]{2,1,0:T(8,128)}, s32[]{:T(128)}, f32[4,64]{1,0:T(4,128)S(1)}, ...), condition=%wide.region_12.13_spmd.clone, body=%wide.region_11.12_spmd.clone.sunk | while | flops 2097160 | bytes 6292391 | solution.py:25
  494.3 9.8 fusion.94
  511.2 15.7 %fusion.31 = f32[256,64,64]{0,2,1:T(8,128)} fusion(f32[256,64,64]{0,2,1:T(8,128)S(1)} %get-tuple-element.503, f32[256,64,64]{0,2,1:T(8,128)S(1)} %copy-done.7, f32[64]{0:T(128)S(1)} %copy-done.73, f32[256,64]{0,1:T(8,128)S(1)} %get-tuple-element.490, f32[256,64]{0,1:T(8,128)S(1)} %copy-done.43, f32[256,256]{1,0:T(8,128)S(1)} %copy-done.24, ...), kind=kOutput, calls=%fused_computation.61 | convolution fusion | flops 3242196992 | bytes 13107456 | tf_op jit(solution)/shard_map/transpose(jvp(tsh,shp->thp))/dot_general | solution.py:44
  526.9 6.0 copy.274
  532.9 12.2 multiply_reduce_fusion.4
  550.2 7.2 pad_add_fusion
  567.0 6.1 reshape.444
  573.1 15.8 %concatenate.35 = f32[259,4,2128]{2,1,0:T(4,128)} concatenate(f32[259,4,1024]{2,1,0:T(4,128)} %copy.282, f32[259,4,1024]{2,1,0:T(4,128)} %reshape.444, f32[259,4,32]{2,1,0:T(4,128)S(1)} %copy.283, f32[259,4,32]{2,1,0:T(4,128)S(1)} %copy.284, f32[259,4,16]{2,1,0:T(4,128)S(1)} %copy.285), dimensions={2} | concatenate | bytes 17636864 | tf_op jit(solution)/shard_map/concatenate | solution.py:243
  588.9 11.4 reshape.453
  600.3 27.3 %copy.286 = f32[1,259,8512]{1,0,2:T(1,128)} copy(f32[1,259,8512]{2,1,0:T(8,128)} %reshape.453) | data formatting | bytes 17636864 | tf_op jit(solution)/shard_map/reshape | solution.py:243
  627.6 6.5 all-to-all-start.3
  635.4 140.7 %all-to-all-done.3 = f32[1,259,8512]{1,0,2:T(1,128)} async-done(((f32[1,259,8512]{1,0,2:T(1,128)}), f32[1,259,8512]{1,0,2:T(1,128)}, u32[]{:S(2)}, u32[]{:S(2)}) %all-to-all-start.3) | async-done | bytes 8818464 | tf_op jit(solution)/shard_map/all_to_all | solution.py:246
  776.1 11.9 copy.293
  788.0 7.0 slice.233
  803.2 22.9 %scatter-add.4 = f32[4,256,2128]{1,2,0:T(8,128)} dynamic-update-slice(f32[4,256,2128]{1,2,0:T(8,128)} %copy-done.8, f32[3,3,2128]{1,2,0:T(8,128)S(1)} %add_select_fusion, s32[]{:T(128)} %bitcast.54, s32[]{:T(128)} %bitcast.55, s32[]{:T(128)} %constant.140.clone.1) | dynamic-update-slice | bytes 153220 | tf_op jit(solution)/shard_map/scatter-add | solution.py:248
  826.1 5.9 convert_element_type.125
  832.0 6.4 copy.289
  838.4 15.7 %fusion.155 = f32[1024,2048]{1,0:T(8,128)} fusion(bf16[1024,2128]{1,0:T(8,128)(2,1)} %bitcast.325, bf16[2048,2128]{1,0:T(8,128)(2,1)} %concatenate.29), kind=kOutput, calls=%fused_computation.251 | convolution fusion | flops 8925478912 | bytes 21463040 | tf_op jit(solution)/shard_map/dot_general | solution.py:251
  858.5 49.7 %all_to_all.52 = bf16[256,4,1024]{0,2,1:T(8,128)(2,1)S(1)} all-to-all(bf16[256,4,1024]{0,2,1:T(8,128)(2,1)S(1)} %fusion.48), channel_id=1, replica_groups=mesh['dp'=8,'tp'=4] {'tp'}, dimensions={1} | all-to-all | bytes 4194304 | tf_op jit(solution)/shard_map/all_to_all | solution.py:194
  910.6 10.7 fusion.154
  922.9 9.1 convolution_bitcast_fusion
  932.0 12.9 fusion.156
  944.9 16.0 %pad_maximum_fusion = f32[2048,3152]{0,1:T(8,128)} fusion(f32[2048,1024]{0,1:T(8,128)} %convolution_bitcast_fusion, f32[2048,2128]{0,1:T(8,128)S(1)} %fusion.156), kind=kLoop, calls=%fused_computation.6 | loop fusion | flops 6455296 | bytes 51642368 | tf_op jit(solution)/shard_map/concatenate | solution.py:265
  966.4 41.9 %all-reduce.16 = (f32[2048]{0:T(1024)}, f32[4352]{0:T(1024)}, f32[64]{0:T(128)}, f32[64]{0:T(128)}, f32[64]{0:T(128)}, /*index=5*/f32[4096]{0:T(1024)}) all-reduce(f32[2048]{0:T(1024)S(1)} %get-tuple-element.425, f32[4352]{0:T(1024)S(1)} %copy-done.32, f32[64]{0:T(128)S(1)} %get-tuple-element.461, ...), channel_id=1, replica_groups=mesh['dp'=8,'tp'=4] {'dp','tp'}, use_global_device_ids=true, to_apply=%region_30.31 | all-reduce | flops 10688 | bytes 85504 | tf_op jit(solution)/shard_map/psum | solution.py:284
  1008.3 46.4 %reduce-scatter.4.cloned.1.call-done = f32[256,2048]{1,0:T(8,128)} async-done(((f32[1024,2048]{1,0:T(8,128)}), f32[256,2048]{1,0:T(8,128)}) %reduce-scatter.4.cloned.1.call-update) | async-done | bytes 2097168 | tf_op jit(solution)/shard_map/reduce_scatter | solution.py:195
  1059.0 249.3 %reduce-scatter.8.cloned.1.call-done = f32[256,3152]{0,1:T(8,128)} async-done(((f32[2048,3152]{0,1:T(8,128)}), f32[256,3152]{0,1:T(8,128)}) %reduce-scatter.8.cloned.1.call-update) | async-done | bytes 3227664 | tf_op jit(solution)/shard_map/reduce_scatter | solution.py:264
  1316.7 118.6 %all-reduce.19.cloned.1.call-done = f32[4352,4]{0,1:T(4,128)} async-done(((f32[4352,4]{0,1:T(4,128)}), f32[4352,4]{0,1:T(4,128)}) %all-reduce.19.cloned.1.call-update) | async-done | bytes 69648 | tf_op jit(solution)/shard_map/psum | solution.py:284
  (294 shorter events, 187.6 us)
Async XLA Ops:
  7.2 59.1 %all-gather.8.cloned.1.call-start = ((), (), s32[]{:S(2)}) async-start(), calls=%async_computation.7 | async-start | bytes 5242880 | tf_op jit(solution)/shard_map/all_gather | solution.py:115
  106.7 6.4 copy-start.74
  106.7 6.4 copy-start.72
  106.7 8.6 copy-start.38
  106.7 72.0 %all-to-all-start = ((bf16[4,1,259,2128]{3,2,1,0:T(8,128)(2,1)}), bf16[4,1,259,2128]{3,2,1,0:T(8,128)(2,1)}, u32[]{:S(2)}, u32[]{:S(2)}) async-start(bf16[4,1,259,2128]{3,2,1,0:T(8,128)(2,1)} %pad_maximum_fusion.1), calls=%async_computation | async-start | bytes 9191424 | tf_op jit(solution)/shard_map/all_to_all | solution.py:121
  111.8 114.3 %all-gather.10.cloned.1.call-start = ((), (), s32[]{:S(2)}) async-start(), calls=%async_computation.9 | async-start | bytes 5242880 | tf_op jit(solution)/shard_map/all_gather | solution.py:202
  112.5 226.7 %all-gather.12.cloned.1.call-start = ((), (), s32[]{:S(2)}) async-start(), calls=%async_computation.13 | async-start | bytes 10485760 | tf_op jit(solution)/shard_map/all_gather | solution.py:12
  113.1 80.9 %copy-start.68 = (f32[64]{0:T(128)}, f32[64]{0:T(128)S(1)}, u32[]{:S(2)}) copy-start(f32[64]{0:T(128)S(1)} %exp.58) | copy-start | bytes 772
  113.4 73.5 %copy-start.45 = (s32[259]{0:T(512)}, s32[259]{0:T(512)S(1)}, u32[]{:S(2)}) copy-start(s32[259]{0:T(512)S(1)} %convert_reduce_fusion) | copy-start | bytes 3112
  186.9 7.2 copy-start.59
  194.1 24.8 %copy-start.20 = (bf16[256,4,16]{0,2,1:T(8,128)(2,1)}, bf16[256,4,16]{0,2,1:T(8,128)(2,1)S(1)}, u32[]{:S(2)}) copy-start(bf16[256,4,16]{0,2,1:T(8,128)(2,1)S(1)} %slice.224) | copy-start | bytes 98308
  212.8 6.1 copy-start.50
  212.8 6.1 copy-start.60
  212.8 6.1 copy-start.64
  218.8 7.2 copy-start.62
  219.0 133.2 %copy-start.42 = (f32[256,64]{0,1:T(8,128)}, f32[256,64]{0,1:T(8,128)S(1)}, u32[]{:S(2)}) copy-start(f32[256,64]{0,1:T(8,128)S(1)} %get-tuple-element.491) | copy-start | bytes 196612
  234.1 7.2 copy-start.46
  234.1 7.2 copy-start.27
  236.7 48.2 %all-to-all-start.2 = ((bf16[4,256,1024]{1,2,0:T(8,128)(2,1)}), bf16[4,256,1024]{1,2,0:T(8,128)(2,1)}, u32[]{:S(2)}, u32[]{:S(2)}) async-start(bf16[4,256,1024]{1,2,0:T(8,128)(2,1)} %copy.273), calls=%async_computation.3 | async-start | bytes 4194304 | tf_op jit(solution)/shard_map/all_to_all | solution.py:206
  241.2 238.3 %all-gather.14.cloned.1.call-start = ((), (), s32[]{:S(2)}) async-start(), calls=%async_computation.14 | async-start | bytes 10485760 | tf_op jit(solution)/shard_map/all_gather | solution.py:12
  241.5 185.7 %copy-start.40 = (pred[256,256]{1,0:T(8,128)(4,1)}, pred[256,256]{1,0:T(8,128)(4,1)S(1)}, u32[]{:S(2)}) copy-start(pred[256,256]{1,0:T(8,128)(4,1)S(1)} %fusion.102) | copy-start | bytes 196612
  296.4 55.8 %copy-start.22 = (f32[256,256]{1,0:T(8,128)}, f32[256,256]{1,0:T(8,128)S(1)}, u32[]{:S(2)}) copy-start(f32[256,256]{1,0:T(8,128)S(1)} %fusion.113) | copy-start | bytes 786436
  352.2 23.7 %copy-start.16 = (f32[256,64,64]{0,2,1:T(8,128)}, f32[256,64,64]{0,2,1:T(8,128)S(1)}, u32[]{:S(2)}) copy-start(f32[256,64,64]{0,2,1:T(8,128)S(1)} %fusion.107) | copy-start | bytes 12582916
  352.2 23.6 %copy-start.11 = (f32[4,256,1024]{1,2,0:T(8,128)S(1)}, f32[4,256,1024]{1,2,0:T(8,128)}, u32[]{:S(2)}) copy-start(f32[4,256,1024]{1,2,0:T(8,128)} %convert_element_type.132) | copy-start | bytes 12582916
  375.9 18.6 %copy-start.47 = (f32[256]{0:T(256)}, f32[256]{0:T(256)S(1)}, u32[]{:S(2)}) copy-start(f32[256]{0:T(256)S(1)} %fusion.139) | copy-start | bytes 3076
  411.7 8.8 copy-start.6
  420.5 6.7 copy-start.3
  420.5 6.7 copy-start.23
  420.5 6.7 copy-start.43
  494.3 9.9 copy-start.1
  494.3 9.9 copy-start.4
  526.9 6.0 copy-start.52
  526.9 6.0 copy-start.54
  526.9 6.0 copy-start.56
  550.1 7.2 copy-start.21
  550.1 7.2 copy-start.61
  550.1 7.2 copy-start.63
  550.1 7.2 copy-start.65
  550.1 10.6 copy-start.44
  550.2 10.6 copy-start.69
  627.5 7.1 copy-start.71
  627.6 148.5 %all-to-all-start.3 = ((f32[1,259,8512]{1,0,2:T(1,128)}), f32[1,259,8512]{1,0,2:T(1,128)}, u32[]{:S(2)}, u32[]{:S(2)}) async-start(f32[1,259,8512]{1,0,2:T(1,128)} %copy.286), calls=%async_computation.4 | async-start | bytes 26148864 | tf_op jit(solution)/shard_map/all_to_all | solution.py:246
  634.0 329.9 %reduce-scatter.6.cloned.1.call-start = ((), (), s32[]{:S(2)}) async-start(), calls=%async_computation.10 | async-start | bytes 10485760 | tf_op jit(solution)/shard_map/reduce_scatter | solution.py:250
  854.2 200.5 %reduce-scatter.4.cloned.1.call-start = ((), (), s32[]{:S(2)}) async-start(), calls=%async_computation.8 | async-start | bytes 10485760 | tf_op jit(solution)/shard_map/reduce_scatter | solution.py:195
  921.3 387.0 %reduce-scatter.8.cloned.1.call-start = ((), (), s32[]{:S(2)}) async-start(), calls=%async_computation.11 | async-start | bytes 29048832 | tf_op jit(solution)/shard_map/reduce_scatter | solution.py:264
  961.0 5.4 copy-start.32
  961.1 474.2 %all-reduce.19.cloned.1.call-start = ((), (), s32[]{:S(2)}) async-start(), calls=%async_computation.12 | async-start | bytes 139264 | tf_op jit(solution)/shard_map/psum | solution.py:284
  964.0 90.7 %copy-start.18 = (f32[256,2048]{1,0:T(8,128)S(1)}, f32[256,2048]{1,0:T(8,128)}, u32[]{:S(2)}) copy-start(f32[256,2048]{1,0:T(8,128)} %reduce-scatter.6.cloned.1.call-done) | copy-start | bytes 6291460
  (39 other events, 99.8 us)
Sparse Core Ops, SparseCore 0:
  11.5 54.7 all-gather.7
  114.4 83.3 all-gather.9
  226.2 113.0 all-gather.11
  391.8 87.6 all-gather.13
  854.3 109.6 reduce-scatter.5
  967.2 87.4 reduce-scatter.3
  1057.1 251.1 reduce-scatter.7
  1315.4 119.8 all-reduce.18
